TPU v7x, 512 devices: a whole 4x4x16 slice. The times are simulated.
512 devices in a mesh: fine: 128 (over y, z, core), tele: 4 (over x).
Axes of the slice: x: 4, y: 4, z: 16, core: 2. Of those that a mesh axis runs over, the one named last changes fastest.
Arguments:
- right_side: float32 [8192, 320], P(('fine', 'tele')), may hold values from -6 to 6
- fine_inverse: bfloat16 [8192, 320, 320], P(('fine', 'tele')), may hold values from -0.08 to 0.45
- fine_links: int32 [8192, 6], P(('fine', 'tele')), may hold values from -1 to 8191, as said below
- fine_faces: int32 [8192, 6], P(('fine', 'tele')), may hold values from 0 to 23
- coarse_inverse: bfloat16 [1024, 320, 320], P(('fine', 'tele')), may hold values from -0.04 to 0.21
- coarse_links: int32 [1024, 6], P(('fine', 'tele')), may hold values from -1 to 1023, as said below
- coarse_faces: int32 [1024, 6], P(('fine', 'tele')), may hold values from 0 to 23
- face_operators: bfloat16 [24, 80, 80], replicated, may hold values from -1.25 to 1.25
- agglomerate: int32 [8192], P(('fine', 'tele')), may hold values from 0 to 1023, as said below
Outputs:
- solution: float32 [8192, 320], P(('fine', 'tele'))
Inputs may be any that keep to these rules, and one draw needn't show every extreme that they name: `fine_links`: any entry other than -1 is an element held by the same device as the element, or by the device just before or after it in the order of fine+tele, cyclically. `coarse_links`: coarse elements form blocks of 8 consecutive ones; any entry other than -1 lies in the element's own block or in the block just before or after it, cyclically. `agglomerate`: fine element i maps into block i // 64 of 8 consecutive coarse elements; every coarse element collects exactly 8 fine elements.
All inputs are finite; a program needn't handle non-finite values.
Results may differ from a plain program's by a relative error of at most 0.02.
Values may be sent and summed in bfloat16 or wider, within the bound.
No kernel may reach another device: no remote copies, remote signals or barrier semaphores. Data moves between devices by JAX's collectives and lax.ppermute only.
A program may use at most 64 MiB of HBM per device.

v0:
```python
import jax
import jax.numpy as jnp
from jax import lax
from jax.sharding import PartitionSpec as P

FIELDS = 5
NODES = 4
SWEEPS = 3
CYCLES = 2
OPPOSITE = (1, 0, 3, 2, 5, 4)


def passed_along(block, axis, distance):
    devices = range(lax.axis_size(axis))
    route = [((i - distance) % len(devices), i) for i in devices]
    return lax.ppermute(block, axis, route)


def face_table():
    face_size = NODES * NODES
    column = jnp.arange(6 * FIELDS * face_size, dtype=jnp.int32)
    face_index = column // (FIELDS * face_size)
    within = column % (FIELDS * face_size)
    field_index = within // face_size
    first = within // NODES % NODES
    second = within % NODES
    far_node = NODES - 1
    side = jnp.where(face_index % 2 == 0, 0, far_node)
    node_a = jnp.where(face_index < 2, side, first)
    node_b = jnp.where(face_index < 2, first, jnp.where(face_index < 4, side, second))
    node_c = jnp.where(face_index < 4, second, side)
    target = ((field_index * NODES + node_a) * NODES + node_b) * NODES + node_c
    dof_index = jnp.arange(FIELDS * NODES * NODES * NODES, dtype=jnp.int32)
    return (dof_index[:, None] == target[None, :]).astype(jnp.float32)


def take_traces(field_state, table):
    row_count = field_state.shape[0]
    picked = jnp.dot(
        field_state, table, precision=lax.Precision.HIGHEST, preferred_element_type=jnp.float32
    )
    return picked.astype(jnp.bfloat16).reshape(row_count, 6, -1)


def lift_faces(coupled, table):
    return lax.dot_general(
        coupled,
        table,
        (((1,), (1,)), ((), ())),
        precision=lax.Precision.HIGHEST,
        preferred_element_type=jnp.float32,
    )


def neighbour_rows(preceding, own_traces, following, links, position, row_count, devices):
    trace_pool = jnp.concatenate([preceding, own_traces, following], axis=0).reshape(
        -1, own_traces.shape[2]
    )
    clamped = jnp.maximum(links, 0)
    relative = (clamped // row_count - position + 1) % devices
    opposite = jnp.array(OPPOSITE, jnp.int32)
    row_index = (relative * row_count + clamped % row_count) * 6 + opposite[None, :]
    face_rows = jnp.take(trace_pool, row_index.reshape(-1), axis=0).reshape(links.shape[0], 6, -1)
    return jnp.where((links >= 0)[:, :, None], face_rows, jnp.zeros_like(face_rows))


def face_apply(face_operators, face_rows, faces, table):
    flat_rows = face_rows.reshape(-1, face_rows.shape[2])
    face_kinds = faces.reshape(-1)
    products = jnp.einsum(
        "rk,qjk->rqj", flat_rows, face_operators, preferred_element_type=jnp.float32
    )
    picked = face_kinds[:, None] == jnp.arange(face_operators.shape[0], dtype=jnp.int32)[None, :]
    result = jnp.sum(jnp.where(picked[:, :, None], products, 0.0), axis=1)
    return lift_faces(result.reshape(face_rows.shape[0], -1), table)


def fine_coupling(field_state, face_operators, links, faces, position, devices, table):
    own_traces = take_traces(field_state, table)
    preceding = passed_along(own_traces, ("fine", "tele"), 1)
    following = passed_along(own_traces, ("fine", "tele"), -1)
    face_rows = neighbour_rows(
        preceding, own_traces, following, links, position, field_state.shape[0], devices
    )
    return face_apply(face_operators, face_rows, faces, table)


def coarse_coupling(column_traces, face_operators, links, faces, position, devices, table):
    preceding = passed_along(column_traces, "fine", 1)
    following = passed_along(column_traces, "fine", -1)
    face_rows = neighbour_rows(
        preceding, column_traces, following, links, position, column_traces.shape[0], devices
    )
    return face_apply(face_operators, face_rows, faces, table)


def apply_inverse(inverse, lowered):
    return jnp.einsum("nij,nj->ni", inverse, lowered, preferred_element_type=jnp.float32)


def shards(
    right_side,
    fine_inverse,
    fine_links,
    fine_faces,
    coarse_inverse,
    coarse_links,
    coarse_faces,
    face_operators,
    agglomerate,
):
    table = face_table()
    tele_size = lax.axis_size("tele")
    fine_position = lax.axis_index("fine") * tele_size + lax.axis_index("tele")
    fine_devices = lax.axis_size("fine") * tele_size
    column_position = lax.axis_index("fine")
    columns = lax.axis_size("fine")
    column_rows = coarse_inverse.shape[0] * tele_size
    local_target = agglomerate % column_rows
    member = (local_target[:, None] == jnp.arange(column_rows, dtype=jnp.int32)[None, :]).astype(
        jnp.float32
    )
    block_inverse = lax.all_gather(coarse_inverse, "tele", axis=0, tiled=True)
    index_lists = lax.all_gather(
        jnp.concatenate([coarse_links, coarse_faces], axis=1), "tele", axis=0, tiled=True
    )
    block_links = index_lists[:, :6]
    block_faces = index_lists[:, 6:]
    solution = jnp.zeros(right_side.shape, jnp.float32)
    for cycle_index in range(CYCLES):
        for sweep_index in range(SWEEPS):
            if cycle_index == 0 and sweep_index == 0:
                coupled = jnp.zeros(right_side.shape, jnp.float32)
            else:
                coupled = fine_coupling(
                    solution,
                    face_operators,
                    fine_links,
                    fine_faces,
                    fine_position,
                    fine_devices,
                    table,
                )
            lowered = (right_side - coupled).astype(jnp.bfloat16)
            solution = apply_inverse(fine_inverse, lowered)
        residual = lowered.astype(jnp.float32) - fine_coupling(
            solution, face_operators, fine_links, fine_faces, fine_position, fine_devices, table
        )
        partial_sum = jnp.dot(
            member.T, residual, precision=lax.Precision.HIGHEST, preferred_element_type=jnp.float32
        )
        restricted = lax.psum(partial_sum, "tele")
        coarse_state = apply_inverse(block_inverse, restricted.astype(jnp.bfloat16))
        for sweep_index in range(SWEEPS - 1):
            coupled_coarse = coarse_coupling(
                take_traces(coarse_state, table),
                face_operators,
                block_links,
                block_faces,
                column_position,
                columns,
                table,
            )
            coarse_state = apply_inverse(
                block_inverse, (restricted - coupled_coarse).astype(jnp.bfloat16)
            )
        solution = solution + jnp.take(coarse_state, local_target, axis=0)
    return solution


def solution(mesh):
    return jax.shard_map(
        shards,
        mesh=mesh,
        in_specs=(
            P(("fine", "tele"), None),
            P(("fine", "tele"), None, None),
            P(("fine", "tele"), None),
            P(("fine", "tele"), None),
            P(("fine", "tele"), None, None),
            P(("fine", "tele"), None),
            P(("fine", "tele"), None),
            P(),
            P(("fine", "tele")),
        ),
        out_specs=P(("fine", "tele"), None),
        check_vma=False,
    )
```

profile of v0, /device:TPU:2, one launch (start us, length us, event | category | flops | bytes accessed | tf_op | source)
XLA Modules:
  0.0 242.5 jit_solution(18185007734287332940)
XLA Ops:
  6.7 0.9 convert_bitcast_fusion
  7.5 3.3 %fusion.76 = f32[16,1,320]{2,1,0:T(1,128)S(1)} fusion(bf16[16,320,320]{2,1,0:T(8,128)(2,1)} %param.27, bf16[16,320,1]{1,0,2:T(8,128)(2,1)S(1)} %convert_bitcast_fusion), kind=kOutput, calls=%fused_computation.136 | convolution fusion | flops 3276800 | bytes 3307520 | tf_op jit(solution)/shard_map/nij,nj->ni/dot_general | solution.py:98
  11.3 7.8 %collective-permute-start.1 = (bf16[16,6,80]{2,1,0:T(8,128)(2,1)S(1)}, bf16[16,6,80]{2,1,0:T(8,128)(2,1)S(1)}, u32[]{:S(2)}, u32[]{:S(2)}) collective-permute-start(bf16[16,6,80]{2,1,0:T(8,128)(2,1)S(1)} %reshape.333), channel_id=1, source_target_pairs={{1,0},{2,1},{3,2},{4,3},{5,4},{6,5},{7,6},{8,7},{9,8},{10,9},{11,1... | collective-permute-start | bytes 46088 | tf_op jit(solution)/shard_map/ppermute | solution.py:16
  19.1 1.9 collective-permute-start
  21.2 15.2 %all-gather = s32[4,2,12]{2,1,0:T(2,128)S(1)} all-gather(s32[1,2,12]{2,1,0:T(2,128)S(1)} %add_bitcast_fusion), channel_id=1, replica_groups=mesh['fine'=128,'tele'=4] {'tele'}, dimensions={0}, use_global_device_ids=true | all-gather | bytes 480 | tf_op jit(solution)/shard_map/all_gather | solution.py:124
  37.4 0.7 gather_fusion
  39.0 3.5 %fusion.73 = f32[16,1,320]{2,1,0:T(1,128)S(1)} fusion(bf16[16,320,320]{2,1,0:T(8,128)(2,1)} %param.27, bf16[16,320,1]{1,0,2:T(8,128)(2,1)S(1)} %fusion.18), kind=kOutput, calls=%fused_computation.133 | convolution fusion | flops 3276800 | bytes 3307520 | tf_op jit(solution)/shard_map/nij,nj->ni/dot_general | solution.py:98
  43.0 2.6 %collective-permute-start.3 = (bf16[16,6,80]{2,1,0:T(8,128)(2,1)S(1)}, bf16[16,6,80]{2,1,0:T(8,128)(2,1)S(1)}, u32[]{:S(2)}, u32[]{:S(2)}) collective-permute-start(bf16[16,6,80]{2,1,0:T(8,128)(2,1)S(1)} %reshape.337), channel_id=1, source_target_pairs={{1,0},{2,1},{3,2},{4,3},{5,4},{6,5},{7,6},{8,7},{9,8},{10,9},{11,1... | collective-permute-start | bytes 46088 | tf_op jit(solution)/shard_map/ppermute | solution.py:16
  45.5 3.3 %collective-permute-start.2 = (bf16[16,6,80]{2,1,0:T(8,128)(2,1)S(1)}, bf16[16,6,80]{2,1,0:T(8,128)(2,1)S(1)}, u32[]{:S(2)}, u32[]{:S(2)}) collective-permute-start(bf16[16,6,80]{2,1,0:T(8,128)(2,1)S(1)} %reshape.337), channel_id=1, source_target_pairs={{511,0},{0,1},{1,2},{2,3},{3,4},{4,5},{5,6},{6,7},{7,8},{8,9},{9,1... | collective-permute-start | bytes 46088 | tf_op jit(solution)/shard_map/ppermute | solution.py:16
  49.5 4.9 %collective-permute-done.2 = bf16[16,6,80]{2,1,0:T(8,128)(2,1)S(1)} collective-permute-done((bf16[16,6,80]{2,1,0:T(8,128)(2,1)S(1)}, bf16[16,6,80]{2,1,0:T(8,128)(2,1)S(1)}, u32[]{:S(2)}, u32[]{:S(2)}) %collective-permute-start.2) | collective-permute-done | bytes 15392 | tf_op jit(solution)/shard_map/ppermute | solution.py:16
  56.0 3.3 %fusion.70 = f32[16,1,320]{2,1,0:T(1,128)S(1)} fusion(bf16[16,320,320]{2,1,0:T(8,128)(2,1)} %param.27, bf16[16,320,1]{1,0,2:T(8,128)(2,1)S(1)} %bitcast.138), kind=kOutput, calls=%fused_computation.130 | convolution fusion | flops 3276800 | bytes 3307520 | tf_op jit(solution)/shard_map/nij,nj->ni/dot_general | solution.py:98
  59.8 8.2 %collective-permute-start.5 = (bf16[16,6,80]{2,1,0:T(8,128)(2,1)S(1)}, bf16[16,6,80]{2,1,0:T(8,128)(2,1)S(1)}, u32[]{:S(2)}, u32[]{:S(2)}) collective-permute-start(bf16[16,6,80]{2,1,0:T(8,128)(2,1)S(1)} %reshape.341), channel_id=1, source_target_pairs={{1,0},{2,1},{3,2},{4,3},{5,4},{6,5},{7,6},{8,7},{9,8},{10,9},{11,1... | collective-permute-start | bytes 46088 | tf_op jit(solution)/shard_map/ppermute | solution.py:16
  68.0 1.9 collective-permute-start.4
  70.0 3.9 %collective-permute-done.4 = bf16[16,6,80]{2,1,0:T(8,128)(2,1)S(1)} collective-permute-done((bf16[16,6,80]{2,1,0:T(8,128)(2,1)S(1)}, bf16[16,6,80]{2,1,0:T(8,128)(2,1)S(1)}, u32[]{:S(2)}, u32[]{:S(2)}) %collective-permute-start.4) | collective-permute-done | bytes 15392 | tf_op jit(solution)/shard_map/ppermute | solution.py:16
  75.8 17.8 %psum.14 = f32[8,320]{1,0:T(8,128)S(1)} all-reduce(f32[8,320]{1,0:T(8,128)S(1)} %fusion.145), channel_id=1, replica_groups=mesh['fine'=128,'tele'=4] {'tele'}, use_global_device_ids=true, to_apply=%region_3.5 | all-reduce | flops 2560 | bytes 20480 | tf_op jit(solution)/shard_map/psum | solution.py:152
  93.6 2.3 fusion.118
  96.3 1.9 collective-permute-start.7
  98.2 2.4 collective-permute-start.6
  100.8 5.9 %collective-permute-done.6 = bf16[8,6,80]{2,1,0:T(8,128)(2,1)S(1)} collective-permute-done((bf16[8,6,80]{2,1,0:T(8,128)(2,1)S(1)}, bf16[8,6,80]{2,1,0:T(8,128)(2,1)S(1)}, u32[]{:S(2)}, u32[]{:S(2)}) %collective-permute-start.6) | collective-permute-done | bytes 7712 | tf_op jit(solution)/shard_map/ppermute | solution.py:16
  108.2 2.3 fusion.115
  110.9 1.9 collective-permute-start.9
  112.8 2.4 collective-permute-start.8
  115.3 5.9 %collective-permute-done.8 = bf16[8,6,80]{2,1,0:T(8,128)(2,1)S(1)} collective-permute-done((bf16[8,6,80]{2,1,0:T(8,128)(2,1)S(1)}, bf16[8,6,80]{2,1,0:T(8,128)(2,1)S(1)}, u32[]{:S(2)}, u32[]{:S(2)}) %collective-permute-start.8) | collective-permute-done | bytes 7712 | tf_op jit(solution)/shard_map/ppermute | solution.py:16
  124.5 3.3 %collective-permute-start.11 = (bf16[16,6,80]{2,1,0:T(8,128)(2,1)S(1)}, bf16[16,6,80]{2,1,0:T(8,128)(2,1)S(1)}, u32[]{:S(2)}, u32[]{:S(2)}) collective-permute-start(bf16[16,6,80]{2,1,0:T(8,128)(2,1)S(1)} %reshape.353), channel_id=1, source_target_pairs={{1,0},{2,1},{3,2},{4,3},{5,4},{6,5},{7,6},{8,7},{9,8},{10,9},{11,1... | collective-permute-start | bytes 46088 | tf_op jit(solution)/shard_map/ppermute | solution.py:16
  127.9 2.5 %collective-permute-start.10 = (bf16[16,6,80]{2,1,0:T(8,128)(2,1)S(1)}, bf16[16,6,80]{2,1,0:T(8,128)(2,1)S(1)}, u32[]{:S(2)}, u32[]{:S(2)}) collective-permute-start(bf16[16,6,80]{2,1,0:T(8,128)(2,1)S(1)} %reshape.353), channel_id=1, source_target_pairs={{511,0},{0,1},{1,2},{2,3},{3,4},{4,5},{5,6},{6,7},{7,8},{8,9},{9,1... | collective-permute-start | bytes 46088 | tf_op jit(solution)/shard_map/ppermute | solution.py:16
  130.4 3.3 %collective-permute-done.10 = bf16[16,6,80]{2,1,0:T(8,128)(2,1)S(1)} collective-permute-done((bf16[16,6,80]{2,1,0:T(8,128)(2,1)S(1)}, bf16[16,6,80]{2,1,0:T(8,128)(2,1)S(1)}, u32[]{:S(2)}, u32[]{:S(2)}) %collective-permute-start.10) | collective-permute-done | bytes 15392 | tf_op jit(solution)/shard_map/ppermute | solution.py:16
  135.4 3.3 %fusion.68 = f32[16,1,320]{2,1,0:T(1,128)S(1)} fusion(bf16[16,320,320]{2,1,0:T(8,128)(2,1)} %param.27, bf16[16,320,1]{1,0,2:T(8,128)(2,1)S(1)} %fusion.17), kind=kOutput, calls=%fused_computation.128 | convolution fusion | flops 3276800 | bytes 3307520 | tf_op jit(solution)/shard_map/nij,nj->ni/dot_general | solution.py:98
  139.1 6.9 %collective-permute-start.13 = (bf16[16,6,80]{2,1,0:T(8,128)(2,1)S(1)}, bf16[16,6,80]{2,1,0:T(8,128)(2,1)S(1)}, u32[]{:S(2)}, u32[]{:S(2)}) collective-permute-start(bf16[16,6,80]{2,1,0:T(8,128)(2,1)S(1)} %reshape.357), channel_id=1, source_target_pairs={{1,0},{2,1},{3,2},{4,3},{5,4},{6,5},{7,6},{8,7},{9,8},{10,9},{11,1... | collective-permute-start | bytes 46088 | tf_op jit(solution)/shard_map/ppermute | solution.py:16
  146.0 2.1 collective-permute-start.12
  148.2 3.7 %collective-permute-done.12 = bf16[16,6,80]{2,1,0:T(8,128)(2,1)S(1)} collective-permute-done((bf16[16,6,80]{2,1,0:T(8,128)(2,1)S(1)}, bf16[16,6,80]{2,1,0:T(8,128)(2,1)S(1)}, u32[]{:S(2)}, u32[]{:S(2)}) %collective-permute-start.12) | collective-permute-done | bytes 15392 | tf_op jit(solution)/shard_map/ppermute | solution.py:16
  153.5 3.3 %fusion.65 = f32[16,1,320]{2,1,0:T(1,128)S(1)} fusion(bf16[16,320,320]{2,1,0:T(8,128)(2,1)} %param.27, bf16[16,320,1]{1,0,2:T(8,128)(2,1)S(1)} %fusion.16), kind=kOutput, calls=%fused_computation.125 | convolution fusion | flops 3276800 | bytes 3307520 | tf_op jit(solution)/shard_map/nij,nj->ni/dot_general | solution.py:98
  157.3 6.8 %collective-permute-start.15 = (bf16[16,6,80]{2,1,0:T(8,128)(2,1)S(1)}, bf16[16,6,80]{2,1,0:T(8,128)(2,1)S(1)}, u32[]{:S(2)}, u32[]{:S(2)}) collective-permute-start(bf16[16,6,80]{2,1,0:T(8,128)(2,1)S(1)} %reshape.361), channel_id=1, source_target_pairs={{1,0},{2,1},{3,2},{4,3},{5,4},{6,5},{7,6},{8,7},{9,8},{10,9},{11,1... | collective-permute-start | bytes 46088 | tf_op jit(solution)/shard_map/ppermute | solution.py:16
  164.1 1.9 collective-permute-start.14
  166.0 3.9 %collective-permute-done.14 = bf16[16,6,80]{2,1,0:T(8,128)(2,1)S(1)} collective-permute-done((bf16[16,6,80]{2,1,0:T(8,128)(2,1)S(1)}, bf16[16,6,80]{2,1,0:T(8,128)(2,1)S(1)}, u32[]{:S(2)}, u32[]{:S(2)}) %collective-permute-start.14) | collective-permute-done | bytes 15392 | tf_op jit(solution)/shard_map/ppermute | solution.py:16
  171.6 3.3 %fusion.62 = f32[16,1,320]{2,1,0:T(1,128)S(1)} fusion(bf16[16,320,320]{2,1,0:T(8,128)(2,1)} %param.27, bf16[16,320,1]{1,0,2:T(8,128)(2,1)S(1)} %bitcast.137), kind=kOutput, calls=%fused_computation.122 | convolution fusion | flops 3276800 | bytes 3307520 | tf_op jit(solution)/shard_map/nij,nj->ni/dot_general | solution.py:98
  175.3 6.8 %collective-permute-start.17 = (bf16[16,6,80]{2,1,0:T(8,128)(2,1)S(1)}, bf16[16,6,80]{2,1,0:T(8,128)(2,1)S(1)}, u32[]{:S(2)}, u32[]{:S(2)}) collective-permute-start(bf16[16,6,80]{2,1,0:T(8,128)(2,1)S(1)} %reshape.365), channel_id=1, source_target_pairs={{1,0},{2,1},{3,2},{4,3},{5,4},{6,5},{7,6},{8,7},{9,8},{10,9},{11,1... | collective-permute-start | bytes 46088 | tf_op jit(solution)/shard_map/ppermute | solution.py:16
  182.1 1.9 collective-permute-start.16
  184.1 3.9 %collective-permute-done.16 = bf16[16,6,80]{2,1,0:T(8,128)(2,1)S(1)} collective-permute-done((bf16[16,6,80]{2,1,0:T(8,128)(2,1)S(1)}, bf16[16,6,80]{2,1,0:T(8,128)(2,1)S(1)}, u32[]{:S(2)}, u32[]{:S(2)}) %collective-permute-start.16) | collective-permute-done | bytes 15392 | tf_op jit(solution)/shard_map/ppermute | solution.py:16
  190.0 17.7 %psum.15 = f32[8,320]{1,0:T(8,128)S(1)} all-reduce(f32[8,320]{1,0:T(8,128)S(1)} %fusion.144), channel_id=1, replica_groups=mesh['fine'=128,'tele'=4] {'tele'}, use_global_device_ids=true, to_apply=%region_10.14 | all-reduce | flops 2560 | bytes 20480 | tf_op jit(solution)/shard_map/psum | solution.py:152
  208.7 1.9 collective-permute-start.19
  210.6 2.4 collective-permute-start.18
  213.1 6.0 %collective-permute-done.18 = bf16[8,6,80]{2,1,0:T(8,128)(2,1)S(1)} collective-permute-done((bf16[8,6,80]{2,1,0:T(8,128)(2,1)S(1)}, bf16[8,6,80]{2,1,0:T(8,128)(2,1)S(1)}, u32[]{:S(2)}, u32[]{:S(2)}) %collective-permute-start.18) | collective-permute-done | bytes 7712 | tf_op jit(solution)/shard_map/ppermute | solution.py:16
  220.6 0.7 fusion.107
  221.8 1.9 collective-permute-start.21
  223.7 2.4 collective-permute-start.20
  226.1 6.0 %collective-permute-done.20 = bf16[8,6,80]{2,1,0:T(8,128)(2,1)S(1)} collective-permute-done((bf16[8,6,80]{2,1,0:T(8,128)(2,1)S(1)}, bf16[8,6,80]{2,1,0:T(8,128)(2,1)S(1)}, u32[]{:S(2)}, u32[]{:S(2)}) %collective-permute-start.20) | collective-permute-done | bytes 7712 | tf_op jit(solution)/shard_map/ppermute | solution.py:16
  233.7 0.7 fusion.104
  235.0 0.7 bitcast_add_fusion
  (163 shorter events, 26.9 us)
Async XLA Ops:
  6.5 31.5 %copy-start = (bf16[24,80,80]{2,1,0:T(8,128)(2,1)S(1)}, bf16[24,80,80]{2,1,0:T(8,128)(2,1)}, u32[]{:S(2)}) copy-start(bf16[24,80,80]{2,1,0:T(8,128)(2,1)} %param.33) | copy-start | bytes 921604
  6.5 29.8 %copy-start.5 = (s32[6]{0:T(128)S(1)}, s32[6]{0:T(128)}, u32[]{:S(2)}) copy-start(s32[6]{0:T(128)} %constant.277.clone) | copy-start | bytes 76
  6.5 32.1 %copy-start.2 = (f32[16,320]{1,0:T(8,128)S(1)}, f32[16,320]{1,0:T(8,128)}, u32[]{:S(2)}) copy-start(f32[16,320]{1,0:T(8,128)} %param.26) | copy-start | bytes 61444
  6.5 14.5 %copy-start.3 = (s32[16,6]{0,1:T(8,128)S(1)}, s32[16,6]{0,1:T(8,128)}, u32[]{:S(2)}) copy-start(s32[16,6]{0,1:T(8,128)} %param.28) | copy-start | bytes 1156
  6.5 14.5 %copy-start.6 = (s32[2,6]{1,0:T(2,128)S(1)}, s32[2,6]{1,0:T(2,128)}, u32[]{:S(2)}) copy-start(s32[2,6]{1,0:T(2,128)} %param.32) | copy-start | bytes 148
  6.5 14.5 %copy-start.7 = (s32[2,6]{1,0:T(2,128)S(1)}, s32[2,6]{1,0:T(2,128)}, u32[]{:S(2)}) copy-start(s32[2,6]{1,0:T(2,128)} %param.31) | copy-start | bytes 148
  6.6 30.1 %copy-start.8 = (s32[16]{0:T(128)S(1)}, s32[16]{0:T(128)}, u32[]{:S(2)}) copy-start(s32[16]{0:T(128)} %param.34) | copy-start | bytes 196
  6.6 30.3 %copy-start.4 = (s32[16,6]{0,1:T(8,128)S(1)}, s32[16,6]{0,1:T(8,128)}, u32[]{:S(2)}) copy-start(s32[16,6]{0,1:T(8,128)} %param.29) | copy-start | bytes 1156
  6.6 87.0 %all-gather.3.cloned.1.call-start = ((), (), s32[]{:S(2)}) async-start(), calls=%async_computation | async-start | bytes 2457600 | tf_op jit(solution)/shard_map/all_gather | solution.py:123
  11.3 26.0 %collective-permute-start.1 = (bf16[16,6,80]{2,1,0:T(8,128)(2,1)S(1)}, bf16[16,6,80]{2,1,0:T(8,128)(2,1)S(1)}, u32[]{:S(2)}, u32[]{:S(2)}) collective-permute-start(bf16[16,6,80]{2,1,0:T(8,128)(2,1)S(1)} %reshape.333), channel_id=1, source_target_pairs={{1,0},{2,1},{3,2},{4,3},{5,4},{6,5},{7,6},{8,7},{9,8},{10,9},{11,1... | collective-permute-start | bytes 46088 | tf_op jit(solution)/shard_map/ppermute | solution.py:16
  19.1 18.2 %collective-permute-start = (bf16[16,6,80]{2,1,0:T(8,128)(2,1)S(1)}, bf16[16,6,80]{2,1,0:T(8,128)(2,1)S(1)}, u32[]{:S(2)}, u32[]{:S(2)}) collective-permute-start(bf16[16,6,80]{2,1,0:T(8,128)(2,1)S(1)} %reshape.333), channel_id=1, source_target_pairs={{511,0},{0,1},{1,2},{2,3},{3,4},{4,5},{5,6},{6,7},{7,8},{8,9},{9,1... | collective-permute-start | bytes 46088 | tf_op jit(solution)/shard_map/ppermute | solution.py:16
  43.0 6.5 %collective-permute-start.3 = (bf16[16,6,80]{2,1,0:T(8,128)(2,1)S(1)}, bf16[16,6,80]{2,1,0:T(8,128)(2,1)S(1)}, u32[]{:S(2)}, u32[]{:S(2)}) collective-permute-start(bf16[16,6,80]{2,1,0:T(8,128)(2,1)S(1)} %reshape.337), channel_id=1, source_target_pairs={{1,0},{2,1},{3,2},{4,3},{5,4},{6,5},{7,6},{8,7},{9,8},{10,9},{11,1... | collective-permute-start | bytes 46088 | tf_op jit(solution)/shard_map/ppermute | solution.py:16
  45.5 8.8 %collective-permute-start.2 = (bf16[16,6,80]{2,1,0:T(8,128)(2,1)S(1)}, bf16[16,6,80]{2,1,0:T(8,128)(2,1)S(1)}, u32[]{:S(2)}, u32[]{:S(2)}) collective-permute-start(bf16[16,6,80]{2,1,0:T(8,128)(2,1)S(1)} %reshape.337), channel_id=1, source_target_pairs={{511,0},{0,1},{1,2},{2,3},{3,4},{4,5},{5,6},{6,7},{7,8},{8,9},{9,1... | collective-permute-start | bytes 46088 | tf_op jit(solution)/shard_map/ppermute | solution.py:16
  59.8 10.2 %collective-permute-start.5 = (bf16[16,6,80]{2,1,0:T(8,128)(2,1)S(1)}, bf16[16,6,80]{2,1,0:T(8,128)(2,1)S(1)}, u32[]{:S(2)}, u32[]{:S(2)}) collective-permute-start(bf16[16,6,80]{2,1,0:T(8,128)(2,1)S(1)} %reshape.341), channel_id=1, source_target_pairs={{1,0},{2,1},{3,2},{4,3},{5,4},{6,5},{7,6},{8,7},{9,8},{10,9},{11,1... | collective-permute-start | bytes 46088 | tf_op jit(solution)/shard_map/ppermute | solution.py:16
  68.0 5.8 %collective-permute-start.4 = (bf16[16,6,80]{2,1,0:T(8,128)(2,1)S(1)}, bf16[16,6,80]{2,1,0:T(8,128)(2,1)S(1)}, u32[]{:S(2)}, u32[]{:S(2)}) collective-permute-start(bf16[16,6,80]{2,1,0:T(8,128)(2,1)S(1)} %reshape.341), channel_id=1, source_target_pairs={{511,0},{0,1},{1,2},{2,3},{3,4},{4,5},{5,6},{6,7},{7,8},{8,9},{9,1... | collective-permute-start | bytes 46088 | tf_op jit(solution)/shard_map/ppermute | solution.py:16
  93.6 29.3 %copy-start.1 = (bf16[8,320,320]{2,1,0:T(8,128)(2,1)S(1)}, bf16[8,320,320]{2,1,0:T(8,128)(2,1)}, u32[]{:S(2)}) copy-start(bf16[8,320,320]{2,1,0:T(8,128)(2,1)} %all-gather.3.cloned.1.call-done) | copy-start | bytes 4915204
  96.3 4.4 %collective-permute-start.7 = (bf16[8,6,80]{2,1,0:T(8,128)(2,1)S(1)}, bf16[8,6,80]{2,1,0:T(8,128)(2,1)S(1)}, u32[]{:S(2)}, u32[]{:S(2)}) collective-permute-start(bf16[8,6,80]{2,1,0:T(8,128)(2,1)S(1)} %reshape.345), channel_id=1, source_target_pairs={{4,0},{8,4},{12,8},{16,12},{20,16},{24,20},{28,24},{32,28},{36,32}... | collective-permute-start | bytes 23048 | tf_op jit(solution)/shard_map/ppermute | solution.py:16
  98.2 8.4 %collective-permute-start.6 = (bf16[8,6,80]{2,1,0:T(8,128)(2,1)S(1)}, bf16[8,6,80]{2,1,0:T(8,128)(2,1)S(1)}, u32[]{:S(2)}, u32[]{:S(2)}) collective-permute-start(bf16[8,6,80]{2,1,0:T(8,128)(2,1)S(1)} %reshape.345), channel_id=1, source_target_pairs={{508,0},{0,4},{4,8},{8,12},{12,16},{16,20},{20,24},{24,28},{28,32}... | collective-permute-start | bytes 23048 | tf_op jit(solution)/shard_map/ppermute | solution.py:16
  110.9 4.4 %collective-permute-start.9 = (bf16[8,6,80]{2,1,0:T(8,128)(2,1)S(1)}, bf16[8,6,80]{2,1,0:T(8,128)(2,1)S(1)}, u32[]{:S(2)}, u32[]{:S(2)}) collective-permute-start(bf16[8,6,80]{2,1,0:T(8,128)(2,1)S(1)} %reshape.349), channel_id=1, source_target_pairs={{4,0},{8,4},{12,8},{16,12},{20,16},{24,20},{28,24},{32,28},{36,32}... | collective-permute-start | bytes 23048 | tf_op jit(solution)/shard_map/ppermute | solution.py:16
  112.8 8.4 %collective-permute-start.8 = (bf16[8,6,80]{2,1,0:T(8,128)(2,1)S(1)}, bf16[8,6,80]{2,1,0:T(8,128)(2,1)S(1)}, u32[]{:S(2)}, u32[]{:S(2)}) collective-permute-start(bf16[8,6,80]{2,1,0:T(8,128)(2,1)S(1)} %reshape.349), channel_id=1, source_target_pairs={{508,0},{0,4},{4,8},{8,12},{12,16},{16,20},{20,24},{24,28},{28,32}... | collective-permute-start | bytes 23048 | tf_op jit(solution)/shard_map/ppermute | solution.py:16
  124.5 5.9 %collective-permute-start.11 = (bf16[16,6,80]{2,1,0:T(8,128)(2,1)S(1)}, bf16[16,6,80]{2,1,0:T(8,128)(2,1)S(1)}, u32[]{:S(2)}, u32[]{:S(2)}) collective-permute-start(bf16[16,6,80]{2,1,0:T(8,128)(2,1)S(1)} %reshape.353), channel_id=1, source_target_pairs={{1,0},{2,1},{3,2},{4,3},{5,4},{6,5},{7,6},{8,7},{9,8},{10,9},{11,1... | collective-permute-start | bytes 46088 | tf_op jit(solution)/shard_map/ppermute | solution.py:16
  127.9 5.8 %collective-permute-start.10 = (bf16[16,6,80]{2,1,0:T(8,128)(2,1)S(1)}, bf16[16,6,80]{2,1,0:T(8,128)(2,1)S(1)}, u32[]{:S(2)}, u32[]{:S(2)}) collective-permute-start(bf16[16,6,80]{2,1,0:T(8,128)(2,1)S(1)} %reshape.353), channel_id=1, source_target_pairs={{511,0},{0,1},{1,2},{2,3},{3,4},{4,5},{5,6},{6,7},{7,8},{8,9},{9,1... | collective-permute-start | bytes 46088 | tf_op jit(solution)/shard_map/ppermute | solution.py:16
  139.1 9.0 %collective-permute-start.13 = (bf16[16,6,80]{2,1,0:T(8,128)(2,1)S(1)}, bf16[16,6,80]{2,1,0:T(8,128)(2,1)S(1)}, u32[]{:S(2)}, u32[]{:S(2)}) collective-permute-start(bf16[16,6,80]{2,1,0:T(8,128)(2,1)S(1)} %reshape.357), channel_id=1, source_target_pairs={{1,0},{2,1},{3,2},{4,3},{5,4},{6,5},{7,6},{8,7},{9,8},{10,9},{11,1... | collective-permute-start | bytes 46088 | tf_op jit(solution)/shard_map/ppermute | solution.py:16
  146.0 5.8 %collective-permute-start.12 = (bf16[16,6,80]{2,1,0:T(8,128)(2,1)S(1)}, bf16[16,6,80]{2,1,0:T(8,128)(2,1)S(1)}, u32[]{:S(2)}, u32[]{:S(2)}) collective-permute-start(bf16[16,6,80]{2,1,0:T(8,128)(2,1)S(1)} %reshape.357), channel_id=1, source_target_pairs={{511,0},{0,1},{1,2},{2,3},{3,4},{4,5},{5,6},{6,7},{7,8},{8,9},{9,1... | collective-permute-start | bytes 46088 | tf_op jit(solution)/shard_map/ppermute | solution.py:16
  157.3 8.7 %collective-permute-start.15 = (bf16[16,6,80]{2,1,0:T(8,128)(2,1)S(1)}, bf16[16,6,80]{2,1,0:T(8,128)(2,1)S(1)}, u32[]{:S(2)}, u32[]{:S(2)}) collective-permute-start(bf16[16,6,80]{2,1,0:T(8,128)(2,1)S(1)} %reshape.361), channel_id=1, source_target_pairs={{1,0},{2,1},{3,2},{4,3},{5,4},{6,5},{7,6},{8,7},{9,8},{10,9},{11,1... | collective-permute-start | bytes 46088 | tf_op jit(solution)/shard_map/ppermute | solution.py:16
  164.1 5.8 %collective-permute-start.14 = (bf16[16,6,80]{2,1,0:T(8,128)(2,1)S(1)}, bf16[16,6,80]{2,1,0:T(8,128)(2,1)S(1)}, u32[]{:S(2)}, u32[]{:S(2)}) collective-permute-start(bf16[16,6,80]{2,1,0:T(8,128)(2,1)S(1)} %reshape.361), channel_id=1, source_target_pairs={{511,0},{0,1},{1,2},{2,3},{3,4},{4,5},{5,6},{6,7},{7,8},{8,9},{9,1... | collective-permute-start | bytes 46088 | tf_op jit(solution)/shard_map/ppermute | solution.py:16
  175.3 8.7 %collective-permute-start.17 = (bf16[16,6,80]{2,1,0:T(8,128)(2,1)S(1)}, bf16[16,6,80]{2,1,0:T(8,128)(2,1)S(1)}, u32[]{:S(2)}, u32[]{:S(2)}) collective-permute-start(bf16[16,6,80]{2,1,0:T(8,128)(2,1)S(1)} %reshape.365), channel_id=1, source_target_pairs={{1,0},{2,1},{3,2},{4,3},{5,4},{6,5},{7,6},{8,7},{9,8},{10,9},{11,1... | collective-permute-start | bytes 46088 | tf_op jit(solution)/shard_map/ppermute | solution.py:16
  182.1 5.9 %collective-permute-start.16 = (bf16[16,6,80]{2,1,0:T(8,128)(2,1)S(1)}, bf16[16,6,80]{2,1,0:T(8,128)(2,1)S(1)}, u32[]{:S(2)}, u32[]{:S(2)}) collective-permute-start(bf16[16,6,80]{2,1,0:T(8,128)(2,1)S(1)} %reshape.365), channel_id=1, source_target_pairs={{511,0},{0,1},{1,2},{2,3},{3,4},{4,5},{5,6},{6,7},{7,8},{8,9},{9,1... | collective-permute-start | bytes 46088 | tf_op jit(solution)/shard_map/ppermute | solution.py:16
  208.7 4.3 %collective-permute-start.19 = (bf16[8,6,80]{2,1,0:T(8,128)(2,1)S(1)}, bf16[8,6,80]{2,1,0:T(8,128)(2,1)S(1)}, u32[]{:S(2)}, u32[]{:S(2)}) collective-permute-start(bf16[8,6,80]{2,1,0:T(8,128)(2,1)S(1)} %reshape.369), channel_id=1, source_target_pairs={{4,0},{8,4},{12,8},{16,12},{20,16},{24,20},{28,24},{32,28},{36,32}... | collective-permute-start | bytes 23048 | tf_op jit(solution)/shard_map/ppermute | solution.py:16
  210.6 8.4 %collective-permute-start.18 = (bf16[8,6,80]{2,1,0:T(8,128)(2,1)S(1)}, bf16[8,6,80]{2,1,0:T(8,128)(2,1)S(1)}, u32[]{:S(2)}, u32[]{:S(2)}) collective-permute-start(bf16[8,6,80]{2,1,0:T(8,128)(2,1)S(1)} %reshape.369), channel_id=1, source_target_pairs={{508,0},{0,4},{4,8},{8,12},{12,16},{16,20},{20,24},{24,28},{28,32}... | collective-permute-start | bytes 23048 | tf_op jit(solution)/shard_map/ppermute | solution.py:16
  221.8 4.3 %collective-permute-start.21 = (bf16[8,6,80]{2,1,0:T(8,128)(2,1)S(1)}, bf16[8,6,80]{2,1,0:T(8,128)(2,1)S(1)}, u32[]{:S(2)}, u32[]{:S(2)}) collective-permute-start(bf16[8,6,80]{2,1,0:T(8,128)(2,1)S(1)} %reshape.373), channel_id=1, source_target_pairs={{4,0},{8,4},{12,8},{16,12},{20,16},{24,20},{28,24},{32,28},{36,32}... | collective-permute-start | bytes 23048 | tf_op jit(solution)/shard_map/ppermute | solution.py:16
  223.7 8.4 %collective-permute-start.20 = (bf16[8,6,80]{2,1,0:T(8,128)(2,1)S(1)}, bf16[8,6,80]{2,1,0:T(8,128)(2,1)S(1)}, u32[]{:S(2)}, u32[]{:S(2)}) collective-permute-start(bf16[8,6,80]{2,1,0:T(8,128)(2,1)S(1)} %reshape.373), channel_id=1, source_target_pairs={{508,0},{0,4},{4,8},{8,12},{12,16},{16,20},{20,24},{24,28},{28,32}... | collective-permute-start | bytes 23048 | tf_op jit(solution)/shard_map/ppermute | solution.py:16
Sparse Core Ops, SparseCore 0:
  21.2 38.3 all-gather.2
where the time goes:
time: 244 us; the launch traced here: 243 us
  starting transfers between devices  75.3 us (31%)
  blocking collectives  50.6 us (21%)
  waiting for transfers between devices  47.8 us (20%)
  matrix products  40.2 us (16%)
  between operations  14.2 us (6%)
  local copies, waits for them, and re-layouts  12.1 us (5%)
    ppermute x22, starting transfers between devices, passed_along(): return lax.ppermute(block, axis, route)  75.3 us
    ppermute x22, waiting for transfers between devices, passed_along(): return lax.ppermute(block, axis, route)  47.8 us
    psum x2, blocking collectives, shards(): restricted = lax.psum(partial_sum, 'tele')  35.5 us
    dot_general x12, matrix products, apply_inverse(): jnp.einsum('nij,nj->ni', inverse, lowered, preferred_element_type=jnp.flo...  27.4 us
    all_gather x1, blocking collectives, shards(): lax.all_gather(jnp.concatenate([coarse_links, coarse_faces], axis=1), 'te...  15.2 us
    gather x11, local copies, waits for them, and re-layouts, neighbour_rows(): jnp.take(trace_pool, row_index.reshape(-1), axis=0)  7.19 us
  transfers between devices with their start and end apart: 23, of which 11 were waited for; matrix products, arithmetic and copies ran while one was open for 6% of the time, Pallas kernels for 0%

commit v1 on v0

--- a/solution.py
+++ b/solution.py
@@ -149,7 +149,11 @@
         partial_sum = jnp.dot(
             member.T, residual, precision=lax.Precision.HIGHEST, preferred_element_type=jnp.float32
         )
-        restricted = lax.psum(partial_sum, "tele")
+        restricted = partial_sum
+        for hop in (1, 2):
+            restricted = restricted + lax.ppermute(
+                restricted, "tele", [(dev, dev ^ hop) for dev in range(4)]
+            )
         coarse_state = apply_inverse(block_inverse, restricted.astype(jnp.bfloat16))
         for sweep_index in range(SWEEPS - 1):
             coupled_coarse = coarse_coupling(

time: 244 us -> 239 us (0.980)
  blocking collectives: 50.6 us -> 15.2 us
  starting transfers between devices: 75.3 us -> 92.5 us
  waiting for transfers between devices: 47.8 us -> 61.9 us
    psum x2 -> x0, blocking collectives: 35.5 us -> none  [shards(): restricted = lax.psum(partial_sum, 'tele')]
    ppermute x0 -> x4, starting transfers between devices: none -> 17.4 us  [shards(): lax.ppermute(restricted, 'tele', [(dev, dev ^ hop) for dev in range(4)])]
    ppermute x0 -> x4, waiting for transfers between devices: none -> 13.6 us  [shards(): lax.ppermute(restricted, 'tele', [(dev, dev ^ hop) for dev in range(4)])]
  transfers between devices with their start and end apart: 23 -> 27, of which waited for: 11 -> 15; matrix products, arithmetic and copies ran while one was open for 6% -> 6% of each run, Pallas kernels for 0% -> 0%
where the time goes in v1:
time: 239 us; the launch traced here: 238 us
  starting transfers between devices  92.5 us (39%)
  waiting for transfers between devices  61.9 us (26%)
  matrix products  40.3 us (17%)
  blocking collectives  15.2 us (6%)
  between operations  14.2 us (6%)
  local copies, waits for them, and re-layouts  12.1 us (5%)
    ppermute x22, starting transfers between devices, passed_along(): return lax.ppermute(block, axis, route)  75.1 us
    ppermute x22, waiting for transfers between devices, passed_along(): return lax.ppermute(block, axis, route)  48.3 us
    dot_general x12, matrix products, apply_inverse(): jnp.einsum('nij,nj->ni', inverse, lowered, preferred_element_type=jnp.flo...  27.4 us
    ppermute x4, starting transfers between devices, shards(): lax.ppermute(restricted, 'tele', [(dev, dev ^ hop) for dev in range(4)])  17.4 us
    all_gather x1, blocking collectives, shards(): lax.all_gather(jnp.concatenate([coarse_links, coarse_faces], axis=1), 'te...  15.2 us
    ppermute x4, waiting for transfers between devices, shards(): lax.ppermute(restricted, 'tele', [(dev, dev ^ hop) for dev in range(4)])  13.6 us
    gather x11, local copies, waits for them, and re-layouts, neighbour_rows(): jnp.take(trace_pool, row_index.reshape(-1), axis=0)  7.19 us
  transfers between devices with their start and end apart: 27, of which 15 were waited for; matrix products, arithmetic and copies ran while one was open for 6% of the time, Pallas kernels for 0%

profile of v1, /device:TPU:2, one launch (start us, length us, event | category | flops | bytes accessed | tf_op | source)
XLA Modules:
  0.0 238.4 jit_solution(3548786121792401293)
XLA Ops:
  7.5 3.3 %fusion.76 = f32[16,1,320]{2,1,0:T(1,128)S(1)} fusion(bf16[16,320,320]{2,1,0:T(8,128)(2,1)} %param.27, bf16[16,320,1]{1,0,2:T(8,128)(2,1)S(1)} %convert_bitcast_fusion), kind=kOutput, calls=%fused_computation.136 | convolution fusion | flops 3276800 | bytes 3307520 | tf_op jit(solution)/shard_map/nij,nj->ni/dot_general | solution.py:98
  11.2 7.8 %collective-permute-start.1 = (bf16[16,6,80]{2,1,0:T(8,128)(2,1)S(1)}, bf16[16,6,80]{2,1,0:T(8,128)(2,1)S(1)}, u32[]{:S(2)}, u32[]{:S(2)}) collective-permute-start(bf16[16,6,80]{2,1,0:T(8,128)(2,1)S(1)} %reshape.333), channel_id=1, source_target_pairs={{1,0},{2,1},{3,2},{4,3},{5,4},{6,5},{7,6},{8,7},{9,8},{10,9},{11,1... | collective-permute-start | bytes 46088 | tf_op jit(solution)/shard_map/ppermute | solution.py:16
  19.1 1.9 collective-permute-start
  21.1 15.2 %all-gather = s32[4,2,12]{2,1,0:T(2,128)S(1)} all-gather(s32[1,2,12]{2,1,0:T(2,128)S(1)} %add_bitcast_fusion), channel_id=1, replica_groups=mesh['fine'=128,'tele'=4] {'tele'}, dimensions={0}, use_global_device_ids=true | all-gather | bytes 480 | tf_op jit(solution)/shard_map/all_gather | solution.py:124
  38.9 3.5 %fusion.73 = f32[16,1,320]{2,1,0:T(1,128)S(1)} fusion(bf16[16,320,320]{2,1,0:T(8,128)(2,1)} %param.27, bf16[16,320,1]{1,0,2:T(8,128)(2,1)S(1)} %fusion.18), kind=kOutput, calls=%fused_computation.133 | convolution fusion | flops 3276800 | bytes 3307520 | tf_op jit(solution)/shard_map/nij,nj->ni/dot_general | solution.py:98
  42.9 2.7 %collective-permute-start.3 = (bf16[16,6,80]{2,1,0:T(8,128)(2,1)S(1)}, bf16[16,6,80]{2,1,0:T(8,128)(2,1)S(1)}, u32[]{:S(2)}, u32[]{:S(2)}) collective-permute-start(bf16[16,6,80]{2,1,0:T(8,128)(2,1)S(1)} %reshape.337), channel_id=1, source_target_pairs={{1,0},{2,1},{3,2},{4,3},{5,4},{6,5},{7,6},{8,7},{9,8},{10,9},{11,1... | collective-permute-start | bytes 46088 | tf_op jit(solution)/shard_map/ppermute | solution.py:16
  45.5 3.2 %collective-permute-start.2 = (bf16[16,6,80]{2,1,0:T(8,128)(2,1)S(1)}, bf16[16,6,80]{2,1,0:T(8,128)(2,1)S(1)}, u32[]{:S(2)}, u32[]{:S(2)}) collective-permute-start(bf16[16,6,80]{2,1,0:T(8,128)(2,1)S(1)} %reshape.337), channel_id=1, source_target_pairs={{511,0},{0,1},{1,2},{2,3},{3,4},{4,5},{5,6},{6,7},{7,8},{8,9},{9,1... | collective-permute-start | bytes 46088 | tf_op jit(solution)/shard_map/ppermute | solution.py:16
  49.3 4.9 %collective-permute-done.2 = bf16[16,6,80]{2,1,0:T(8,128)(2,1)S(1)} collective-permute-done((bf16[16,6,80]{2,1,0:T(8,128)(2,1)S(1)}, bf16[16,6,80]{2,1,0:T(8,128)(2,1)S(1)}, u32[]{:S(2)}, u32[]{:S(2)}) %collective-permute-start.2) | collective-permute-done | bytes 15392 | tf_op jit(solution)/shard_map/ppermute | solution.py:16
  55.9 3.3 %fusion.70 = f32[16,1,320]{2,1,0:T(1,128)S(1)} fusion(bf16[16,320,320]{2,1,0:T(8,128)(2,1)} %param.27, bf16[16,320,1]{1,0,2:T(8,128)(2,1)S(1)} %bitcast.137), kind=kOutput, calls=%fused_computation.130 | convolution fusion | flops 3276800 | bytes 3307520 | tf_op jit(solution)/shard_map/nij,nj->ni/dot_general | solution.py:98
  59.7 8.2 %collective-permute-start.5 = (bf16[16,6,80]{2,1,0:T(8,128)(2,1)S(1)}, bf16[16,6,80]{2,1,0:T(8,128)(2,1)S(1)}, u32[]{:S(2)}, u32[]{:S(2)}) collective-permute-start(bf16[16,6,80]{2,1,0:T(8,128)(2,1)S(1)} %reshape.341), channel_id=1, source_target_pairs={{1,0},{2,1},{3,2},{4,3},{5,4},{6,5},{7,6},{8,7},{9,8},{10,9},{11,1... | collective-permute-start | bytes 46088 | tf_op jit(solution)/shard_map/ppermute | solution.py:16
  67.9 1.9 collective-permute-start.4
  69.9 3.8 %collective-permute-done.4 = bf16[16,6,80]{2,1,0:T(8,128)(2,1)S(1)} collective-permute-done((bf16[16,6,80]{2,1,0:T(8,128)(2,1)S(1)}, bf16[16,6,80]{2,1,0:T(8,128)(2,1)S(1)}, u32[]{:S(2)}, u32[]{:S(2)}) %collective-permute-start.4) | collective-permute-done | bytes 15392 | tf_op jit(solution)/shard_map/ppermute | solution.py:16
  75.7 6.8 %collective-permute-start.6 = (f32[8,320]{1,0:T(8,128)S(1)}, f32[8,320]{1,0:T(8,128)S(1)}, u32[]{:S(2)}, u32[]{:S(2)}) collective-permute-start(f32[8,320]{1,0:T(8,128)S(1)} %fusion.145), channel_id=1, source_target_pairs={{0,1},{1,0},{2,3},{3,2},{4,5},{5,4},{6,7},{7,6},{8,9},{9,8},{10,11... | collective-permute-start | bytes 30728 | tf_op jit(solution)/shard_map/ppermute | solution.py:154
  84.1 1.9 collective-permute-start.7
  86.0 5.2 %collective-permute-done.7 = f32[8,320]{1,0:T(8,128)S(1)} collective-permute-done((f32[8,320]{1,0:T(8,128)S(1)}, f32[8,320]{1,0:T(8,128)S(1)}, u32[]{:S(2)}, u32[]{:S(2)}) %collective-permute-start.7) | collective-permute-done | bytes 10272 | tf_op jit(solution)/shard_map/ppermute | solution.py:154
  91.2 2.3 fusion.118
  93.9 1.9 collective-permute-start.9
  95.9 2.4 %collective-permute-start.8 = (bf16[8,6,80]{2,1,0:T(8,128)(2,1)S(1)}, bf16[8,6,80]{2,1,0:T(8,128)(2,1)S(1)}, u32[]{:S(2)}, u32[]{:S(2)}) collective-permute-start(bf16[8,6,80]{2,1,0:T(8,128)(2,1)S(1)} %reshape.345), channel_id=1, source_target_pairs={{508,0},{0,4},{4,8},{8,12},{12,16},{16,20},{20,24},{24,28},{28,32}... | collective-permute-start | bytes 23048 | tf_op jit(solution)/shard_map/ppermute | solution.py:16
  98.4 5.9 %collective-permute-done.8 = bf16[8,6,80]{2,1,0:T(8,128)(2,1)S(1)} collective-permute-done((bf16[8,6,80]{2,1,0:T(8,128)(2,1)S(1)}, bf16[8,6,80]{2,1,0:T(8,128)(2,1)S(1)}, u32[]{:S(2)}, u32[]{:S(2)}) %collective-permute-start.8) | collective-permute-done | bytes 7712 | tf_op jit(solution)/shard_map/ppermute | solution.py:16
  105.8 2.3 fusion.115
  108.5 1.9 collective-permute-start.11
  110.4 2.4 %collective-permute-start.10 = (bf16[8,6,80]{2,1,0:T(8,128)(2,1)S(1)}, bf16[8,6,80]{2,1,0:T(8,128)(2,1)S(1)}, u32[]{:S(2)}, u32[]{:S(2)}) collective-permute-start(bf16[8,6,80]{2,1,0:T(8,128)(2,1)S(1)} %reshape.349), channel_id=1, source_target_pairs={{508,0},{0,4},{4,8},{8,12},{12,16},{16,20},{20,24},{24,28},{28,32}... | collective-permute-start | bytes 23048 | tf_op jit(solution)/shard_map/ppermute | solution.py:16
  112.9 5.9 %collective-permute-done.10 = bf16[8,6,80]{2,1,0:T(8,128)(2,1)S(1)} collective-permute-done((bf16[8,6,80]{2,1,0:T(8,128)(2,1)S(1)}, bf16[8,6,80]{2,1,0:T(8,128)(2,1)S(1)}, u32[]{:S(2)}, u32[]{:S(2)}) %collective-permute-start.10) | collective-permute-done | bytes 7712 | tf_op jit(solution)/shard_map/ppermute | solution.py:16
  122.2 3.9 %collective-permute-start.13 = (bf16[16,6,80]{2,1,0:T(8,128)(2,1)S(1)}, bf16[16,6,80]{2,1,0:T(8,128)(2,1)S(1)}, u32[]{:S(2)}, u32[]{:S(2)}) collective-permute-start(bf16[16,6,80]{2,1,0:T(8,128)(2,1)S(1)} %reshape.353), channel_id=1, source_target_pairs={{1,0},{2,1},{3,2},{4,3},{5,4},{6,5},{7,6},{8,7},{9,8},{10,9},{11,1... | collective-permute-start | bytes 46088 | tf_op jit(solution)/shard_map/ppermute | solution.py:16
  126.1 1.9 collective-permute-start.12
  128.0 3.9 %collective-permute-done.12 = bf16[16,6,80]{2,1,0:T(8,128)(2,1)S(1)} collective-permute-done((bf16[16,6,80]{2,1,0:T(8,128)(2,1)S(1)}, bf16[16,6,80]{2,1,0:T(8,128)(2,1)S(1)}, u32[]{:S(2)}, u32[]{:S(2)}) %collective-permute-start.12) | collective-permute-done | bytes 15392 | tf_op jit(solution)/shard_map/ppermute | solution.py:16
  133.6 3.3 %fusion.68 = f32[16,1,320]{2,1,0:T(1,128)S(1)} fusion(bf16[16,320,320]{2,1,0:T(8,128)(2,1)} %param.27, bf16[16,320,1]{1,0,2:T(8,128)(2,1)S(1)} %fusion.17), kind=kOutput, calls=%fused_computation.128 | convolution fusion | flops 3276800 | bytes 3307520 | tf_op jit(solution)/shard_map/nij,nj->ni/dot_general | solution.py:98
  137.3 6.8 %collective-permute-start.15 = (bf16[16,6,80]{2,1,0:T(8,128)(2,1)S(1)}, bf16[16,6,80]{2,1,0:T(8,128)(2,1)S(1)}, u32[]{:S(2)}, u32[]{:S(2)}) collective-permute-start(bf16[16,6,80]{2,1,0:T(8,128)(2,1)S(1)} %reshape.357), channel_id=1, source_target_pairs={{1,0},{2,1},{3,2},{4,3},{5,4},{6,5},{7,6},{8,7},{9,8},{10,9},{11,1... | collective-permute-start | bytes 46088 | tf_op jit(solution)/shard_map/ppermute | solution.py:16
  144.1 1.9 collective-permute-start.14
  146.1 3.9 %collective-permute-done.14 = bf16[16,6,80]{2,1,0:T(8,128)(2,1)S(1)} collective-permute-done((bf16[16,6,80]{2,1,0:T(8,128)(2,1)S(1)}, bf16[16,6,80]{2,1,0:T(8,128)(2,1)S(1)}, u32[]{:S(2)}, u32[]{:S(2)}) %collective-permute-start.14) | collective-permute-done | bytes 15392 | tf_op jit(solution)/shard_map/ppermute | solution.py:16
  151.6 3.3 %fusion.65 = f32[16,1,320]{2,1,0:T(1,128)S(1)} fusion(bf16[16,320,320]{2,1,0:T(8,128)(2,1)} %param.27, bf16[16,320,1]{1,0,2:T(8,128)(2,1)S(1)} %fusion.16), kind=kOutput, calls=%fused_computation.125 | convolution fusion | flops 3276800 | bytes 3307520 | tf_op jit(solution)/shard_map/nij,nj->ni/dot_general | solution.py:98
  155.4 6.8 %collective-permute-start.17 = (bf16[16,6,80]{2,1,0:T(8,128)(2,1)S(1)}, bf16[16,6,80]{2,1,0:T(8,128)(2,1)S(1)}, u32[]{:S(2)}, u32[]{:S(2)}) collective-permute-start(bf16[16,6,80]{2,1,0:T(8,128)(2,1)S(1)} %reshape.361), channel_id=1, source_target_pairs={{1,0},{2,1},{3,2},{4,3},{5,4},{6,5},{7,6},{8,7},{9,8},{10,9},{11,1... | collective-permute-start | bytes 46088 | tf_op jit(solution)/shard_map/ppermute | solution.py:16
  162.2 2.1 collective-permute-start.16
  164.3 3.7 %collective-permute-done.16 = bf16[16,6,80]{2,1,0:T(8,128)(2,1)S(1)} collective-permute-done((bf16[16,6,80]{2,1,0:T(8,128)(2,1)S(1)}, bf16[16,6,80]{2,1,0:T(8,128)(2,1)S(1)}, u32[]{:S(2)}, u32[]{:S(2)}) %collective-permute-start.16) | collective-permute-done | bytes 15392 | tf_op jit(solution)/shard_map/ppermute | solution.py:16
  169.7 3.3 %fusion.62 = f32[16,1,320]{2,1,0:T(1,128)S(1)} fusion(bf16[16,320,320]{2,1,0:T(8,128)(2,1)} %param.27, bf16[16,320,1]{1,0,2:T(8,128)(2,1)S(1)} %bitcast.138), kind=kOutput, calls=%fused_computation.122 | convolution fusion | flops 3276800 | bytes 3307520 | tf_op jit(solution)/shard_map/nij,nj->ni/dot_general | solution.py:98
  173.4 6.8 %collective-permute-start.19 = (bf16[16,6,80]{2,1,0:T(8,128)(2,1)S(1)}, bf16[16,6,80]{2,1,0:T(8,128)(2,1)S(1)}, u32[]{:S(2)}, u32[]{:S(2)}) collective-permute-start(bf16[16,6,80]{2,1,0:T(8,128)(2,1)S(1)} %reshape.365), channel_id=1, source_target_pairs={{1,0},{2,1},{3,2},{4,3},{5,4},{6,5},{7,6},{8,7},{9,8},{10,9},{11,1... | collective-permute-start | bytes 46088 | tf_op jit(solution)/shard_map/ppermute | solution.py:16
  180.2 1.9 collective-permute-start.18
  182.2 3.9 %collective-permute-done.18 = bf16[16,6,80]{2,1,0:T(8,128)(2,1)S(1)} collective-permute-done((bf16[16,6,80]{2,1,0:T(8,128)(2,1)S(1)}, bf16[16,6,80]{2,1,0:T(8,128)(2,1)S(1)}, u32[]{:S(2)}, u32[]{:S(2)}) %collective-permute-start.18) | collective-permute-done | bytes 15392 | tf_op jit(solution)/shard_map/ppermute | solution.py:16
  188.0 6.8 %collective-permute-start.20 = (f32[8,320]{1,0:T(8,128)S(1)}, f32[8,320]{1,0:T(8,128)S(1)}, u32[]{:S(2)}, u32[]{:S(2)}) collective-permute-start(f32[8,320]{1,0:T(8,128)S(1)} %fusion.144), channel_id=1, source_target_pairs={{0,1},{1,0},{2,3},{3,2},{4,5},{5,4},{6,7},{7,6},{8,9},{9,8},{10,11... | collective-permute-start | bytes 30728 | tf_op jit(solution)/shard_map/ppermute | solution.py:154
  194.8 1.7 collective-permute-done.20
  196.5 1.9 collective-permute-start.21
  198.4 5.2 %collective-permute-done.21 = f32[8,320]{1,0:T(8,128)S(1)} collective-permute-done((f32[8,320]{1,0:T(8,128)S(1)}, f32[8,320]{1,0:T(8,128)S(1)}, u32[]{:S(2)}, u32[]{:S(2)}) %collective-permute-start.21) | collective-permute-done | bytes 10272 | tf_op jit(solution)/shard_map/ppermute | solution.py:154
  204.6 1.9 collective-permute-start.23
  206.5 2.4 %collective-permute-start.22 = (bf16[8,6,80]{2,1,0:T(8,128)(2,1)S(1)}, bf16[8,6,80]{2,1,0:T(8,128)(2,1)S(1)}, u32[]{:S(2)}, u32[]{:S(2)}) collective-permute-start(bf16[8,6,80]{2,1,0:T(8,128)(2,1)S(1)} %reshape.369), channel_id=1, source_target_pairs={{508,0},{0,4},{4,8},{8,12},{12,16},{16,20},{20,24},{24,28},{28,32}... | collective-permute-start | bytes 23048 | tf_op jit(solution)/shard_map/ppermute | solution.py:16
  208.9 6.0 %collective-permute-done.22 = bf16[8,6,80]{2,1,0:T(8,128)(2,1)S(1)} collective-permute-done((bf16[8,6,80]{2,1,0:T(8,128)(2,1)S(1)}, bf16[8,6,80]{2,1,0:T(8,128)(2,1)S(1)}, u32[]{:S(2)}, u32[]{:S(2)}) %collective-permute-start.22) | collective-permute-done | bytes 7712 | tf_op jit(solution)/shard_map/ppermute | solution.py:16
  217.6 1.9 collective-permute-start.25
  219.6 2.4 %collective-permute-start.24 = (bf16[8,6,80]{2,1,0:T(8,128)(2,1)S(1)}, bf16[8,6,80]{2,1,0:T(8,128)(2,1)S(1)}, u32[]{:S(2)}, u32[]{:S(2)}) collective-permute-start(bf16[8,6,80]{2,1,0:T(8,128)(2,1)S(1)} %reshape.373), channel_id=1, source_target_pairs={{508,0},{0,4},{4,8},{8,12},{12,16},{16,20},{20,24},{24,28},{28,32}... | collective-permute-start | bytes 23048 | tf_op jit(solution)/shard_map/ppermute | solution.py:16
  222.0 6.0 %collective-permute-done.24 = bf16[8,6,80]{2,1,0:T(8,128)(2,1)S(1)} collective-permute-done((bf16[8,6,80]{2,1,0:T(8,128)(2,1)S(1)}, bf16[8,6,80]{2,1,0:T(8,128)(2,1)S(1)}, u32[]{:S(2)}, u32[]{:S(2)}) %collective-permute-start.24) | collective-permute-done | bytes 7712 | tf_op jit(solution)/shard_map/ppermute | solution.py:16
  (171 shorter events, 32.2 us)
Async XLA Ops:
  6.5 31.4 %copy-start = (bf16[24,80,80]{2,1,0:T(8,128)(2,1)S(1)}, bf16[24,80,80]{2,1,0:T(8,128)(2,1)}, u32[]{:S(2)}) copy-start(bf16[24,80,80]{2,1,0:T(8,128)(2,1)} %param.33) | copy-start | bytes 921604
  6.5 29.8 %copy-start.5 = (s32[6]{0:T(128)S(1)}, s32[6]{0:T(128)}, u32[]{:S(2)}) copy-start(s32[6]{0:T(128)} %constant.277.clone) | copy-start | bytes 76
  6.5 32.0 %copy-start.2 = (f32[16,320]{1,0:T(8,128)S(1)}, f32[16,320]{1,0:T(8,128)}, u32[]{:S(2)}) copy-start(f32[16,320]{1,0:T(8,128)} %param.26) | copy-start | bytes 61444
  6.5 14.5 %copy-start.3 = (s32[16,6]{0,1:T(8,128)S(1)}, s32[16,6]{0,1:T(8,128)}, u32[]{:S(2)}) copy-start(s32[16,6]{0,1:T(8,128)} %param.28) | copy-start | bytes 1156
  6.5 14.5 %copy-start.6 = (s32[2,6]{1,0:T(2,128)S(1)}, s32[2,6]{1,0:T(2,128)}, u32[]{:S(2)}) copy-start(s32[2,6]{1,0:T(2,128)} %param.32) | copy-start | bytes 148
  6.5 14.5 %copy-start.7 = (s32[2,6]{1,0:T(2,128)S(1)}, s32[2,6]{1,0:T(2,128)}, u32[]{:S(2)}) copy-start(s32[2,6]{1,0:T(2,128)} %param.31) | copy-start | bytes 148
  6.6 30.2 %copy-start.4 = (s32[16,6]{0,1:T(8,128)S(1)}, s32[16,6]{0,1:T(8,128)}, u32[]{:S(2)}) copy-start(s32[16,6]{0,1:T(8,128)} %param.29) | copy-start | bytes 1156
  6.6 84.6 %all-gather.3.cloned.1.call-start = ((), (), s32[]{:S(2)}) async-start(), calls=%async_computation | async-start | bytes 2457600 | tf_op jit(solution)/shard_map/all_gather | solution.py:123
  10.8 37.9 %copy-start.8 = (s32[16]{0:T(128)S(1)}, s32[16]{0:T(128)}, u32[]{:S(2)}) copy-start(s32[16]{0:T(128)} %param.34) | copy-start | bytes 196
  11.2 25.9 %collective-permute-start.1 = (bf16[16,6,80]{2,1,0:T(8,128)(2,1)S(1)}, bf16[16,6,80]{2,1,0:T(8,128)(2,1)S(1)}, u32[]{:S(2)}, u32[]{:S(2)}) collective-permute-start(bf16[16,6,80]{2,1,0:T(8,128)(2,1)S(1)} %reshape.333), channel_id=1, source_target_pairs={{1,0},{2,1},{3,2},{4,3},{5,4},{6,5},{7,6},{8,7},{9,8},{10,9},{11,1... | collective-permute-start | bytes 46088 | tf_op jit(solution)/shard_map/ppermute | solution.py:16
  19.1 18.1 %collective-permute-start = (bf16[16,6,80]{2,1,0:T(8,128)(2,1)S(1)}, bf16[16,6,80]{2,1,0:T(8,128)(2,1)S(1)}, u32[]{:S(2)}, u32[]{:S(2)}) collective-permute-start(bf16[16,6,80]{2,1,0:T(8,128)(2,1)S(1)} %reshape.333), channel_id=1, source_target_pairs={{511,0},{0,1},{1,2},{2,3},{3,4},{4,5},{5,6},{6,7},{7,8},{8,9},{9,1... | collective-permute-start | bytes 46088 | tf_op jit(solution)/shard_map/ppermute | solution.py:16
  42.9 6.5 %collective-permute-start.3 = (bf16[16,6,80]{2,1,0:T(8,128)(2,1)S(1)}, bf16[16,6,80]{2,1,0:T(8,128)(2,1)S(1)}, u32[]{:S(2)}, u32[]{:S(2)}) collective-permute-start(bf16[16,6,80]{2,1,0:T(8,128)(2,1)S(1)} %reshape.337), channel_id=1, source_target_pairs={{1,0},{2,1},{3,2},{4,3},{5,4},{6,5},{7,6},{8,7},{9,8},{10,9},{11,1... | collective-permute-start | bytes 46088 | tf_op jit(solution)/shard_map/ppermute | solution.py:16
  45.5 8.7 %collective-permute-start.2 = (bf16[16,6,80]{2,1,0:T(8,128)(2,1)S(1)}, bf16[16,6,80]{2,1,0:T(8,128)(2,1)S(1)}, u32[]{:S(2)}, u32[]{:S(2)}) collective-permute-start(bf16[16,6,80]{2,1,0:T(8,128)(2,1)S(1)} %reshape.337), channel_id=1, source_target_pairs={{511,0},{0,1},{1,2},{2,3},{3,4},{4,5},{5,6},{6,7},{7,8},{8,9},{9,1... | collective-permute-start | bytes 46088 | tf_op jit(solution)/shard_map/ppermute | solution.py:16
  59.7 10.2 %collective-permute-start.5 = (bf16[16,6,80]{2,1,0:T(8,128)(2,1)S(1)}, bf16[16,6,80]{2,1,0:T(8,128)(2,1)S(1)}, u32[]{:S(2)}, u32[]{:S(2)}) collective-permute-start(bf16[16,6,80]{2,1,0:T(8,128)(2,1)S(1)} %reshape.341), channel_id=1, source_target_pairs={{1,0},{2,1},{3,2},{4,3},{5,4},{6,5},{7,6},{8,7},{9,8},{10,9},{11,1... | collective-permute-start | bytes 46088 | tf_op jit(solution)/shard_map/ppermute | solution.py:16
  67.9 5.8 %collective-permute-start.4 = (bf16[16,6,80]{2,1,0:T(8,128)(2,1)S(1)}, bf16[16,6,80]{2,1,0:T(8,128)(2,1)S(1)}, u32[]{:S(2)}, u32[]{:S(2)}) collective-permute-start(bf16[16,6,80]{2,1,0:T(8,128)(2,1)S(1)} %reshape.341), channel_id=1, source_target_pairs={{511,0},{0,1},{1,2},{2,3},{3,4},{4,5},{5,6},{6,7},{7,8},{8,9},{9,1... | collective-permute-start | bytes 46088 | tf_op jit(solution)/shard_map/ppermute | solution.py:16
  75.7 8.5 %collective-permute-start.6 = (f32[8,320]{1,0:T(8,128)S(1)}, f32[8,320]{1,0:T(8,128)S(1)}, u32[]{:S(2)}, u32[]{:S(2)}) collective-permute-start(f32[8,320]{1,0:T(8,128)S(1)} %fusion.145), channel_id=1, source_target_pairs={{0,1},{1,0},{2,3},{3,2},{4,5},{5,4},{6,7},{7,6},{8,9},{9,8},{10,11... | collective-permute-start | bytes 30728 | tf_op jit(solution)/shard_map/ppermute | solution.py:154
  84.1 7.1 %collective-permute-start.7 = (f32[8,320]{1,0:T(8,128)S(1)}, f32[8,320]{1,0:T(8,128)S(1)}, u32[]{:S(2)}, u32[]{:S(2)}) collective-permute-start(f32[8,320]{1,0:T(8,128)S(1)} %add.601), channel_id=1, source_target_pairs={{0,2},{1,3},{2,0},{3,1},{4,6},{5,7},{6,4},{7,5},{8,10},{9,11},{10,... | collective-permute-start | bytes 30728 | tf_op jit(solution)/shard_map/ppermute | solution.py:154
  91.2 29.3 %copy-start.1 = (bf16[8,320,320]{2,1,0:T(8,128)(2,1)S(1)}, bf16[8,320,320]{2,1,0:T(8,128)(2,1)}, u32[]{:S(2)}) copy-start(bf16[8,320,320]{2,1,0:T(8,128)(2,1)} %all-gather.3.cloned.1.call-done) | copy-start | bytes 4915204
  93.9 4.4 %collective-permute-start.9 = (bf16[8,6,80]{2,1,0:T(8,128)(2,1)S(1)}, bf16[8,6,80]{2,1,0:T(8,128)(2,1)S(1)}, u32[]{:S(2)}, u32[]{:S(2)}) collective-permute-start(bf16[8,6,80]{2,1,0:T(8,128)(2,1)S(1)} %reshape.345), channel_id=1, source_target_pairs={{4,0},{8,4},{12,8},{16,12},{20,16},{24,20},{28,24},{32,28},{36,32}... | collective-permute-start | bytes 23048 | tf_op jit(solution)/shard_map/ppermute | solution.py:16
  95.9 8.4 %collective-permute-start.8 = (bf16[8,6,80]{2,1,0:T(8,128)(2,1)S(1)}, bf16[8,6,80]{2,1,0:T(8,128)(2,1)S(1)}, u32[]{:S(2)}, u32[]{:S(2)}) collective-permute-start(bf16[8,6,80]{2,1,0:T(8,128)(2,1)S(1)} %reshape.345), channel_id=1, source_target_pairs={{508,0},{0,4},{4,8},{8,12},{12,16},{16,20},{20,24},{24,28},{28,32}... | collective-permute-start | bytes 23048 | tf_op jit(solution)/shard_map/ppermute | solution.py:16
  108.5 4.4 %collective-permute-start.11 = (bf16[8,6,80]{2,1,0:T(8,128)(2,1)S(1)}, bf16[8,6,80]{2,1,0:T(8,128)(2,1)S(1)}, u32[]{:S(2)}, u32[]{:S(2)}) collective-permute-start(bf16[8,6,80]{2,1,0:T(8,128)(2,1)S(1)} %reshape.349), channel_id=1, source_target_pairs={{4,0},{8,4},{12,8},{16,12},{20,16},{24,20},{28,24},{32,28},{36,32}... | collective-permute-start | bytes 23048 | tf_op jit(solution)/shard_map/ppermute | solution.py:16
  110.4 8.4 %collective-permute-start.10 = (bf16[8,6,80]{2,1,0:T(8,128)(2,1)S(1)}, bf16[8,6,80]{2,1,0:T(8,128)(2,1)S(1)}, u32[]{:S(2)}, u32[]{:S(2)}) collective-permute-start(bf16[8,6,80]{2,1,0:T(8,128)(2,1)S(1)} %reshape.349), channel_id=1, source_target_pairs={{508,0},{0,4},{4,8},{8,12},{12,16},{16,20},{20,24},{24,28},{28,32}... | collective-permute-start | bytes 23048 | tf_op jit(solution)/shard_map/ppermute | solution.py:16
  122.2 5.9 %collective-permute-start.13 = (bf16[16,6,80]{2,1,0:T(8,128)(2,1)S(1)}, bf16[16,6,80]{2,1,0:T(8,128)(2,1)S(1)}, u32[]{:S(2)}, u32[]{:S(2)}) collective-permute-start(bf16[16,6,80]{2,1,0:T(8,128)(2,1)S(1)} %reshape.353), channel_id=1, source_target_pairs={{1,0},{2,1},{3,2},{4,3},{5,4},{6,5},{7,6},{8,7},{9,8},{10,9},{11,1... | collective-permute-start | bytes 46088 | tf_op jit(solution)/shard_map/ppermute | solution.py:16
  126.1 5.8 %collective-permute-start.12 = (bf16[16,6,80]{2,1,0:T(8,128)(2,1)S(1)}, bf16[16,6,80]{2,1,0:T(8,128)(2,1)S(1)}, u32[]{:S(2)}, u32[]{:S(2)}) collective-permute-start(bf16[16,6,80]{2,1,0:T(8,128)(2,1)S(1)} %reshape.353), channel_id=1, source_target_pairs={{511,0},{0,1},{1,2},{2,3},{3,4},{4,5},{5,6},{6,7},{7,8},{8,9},{9,1... | collective-permute-start | bytes 46088 | tf_op jit(solution)/shard_map/ppermute | solution.py:16
  137.3 8.7 %collective-permute-start.15 = (bf16[16,6,80]{2,1,0:T(8,128)(2,1)S(1)}, bf16[16,6,80]{2,1,0:T(8,128)(2,1)S(1)}, u32[]{:S(2)}, u32[]{:S(2)}) collective-permute-start(bf16[16,6,80]{2,1,0:T(8,128)(2,1)S(1)} %reshape.357), channel_id=1, source_target_pairs={{1,0},{2,1},{3,2},{4,3},{5,4},{6,5},{7,6},{8,7},{9,8},{10,9},{11,1... | collective-permute-start | bytes 46088 | tf_op jit(solution)/shard_map/ppermute | solution.py:16
  144.1 5.8 %collective-permute-start.14 = (bf16[16,6,80]{2,1,0:T(8,128)(2,1)S(1)}, bf16[16,6,80]{2,1,0:T(8,128)(2,1)S(1)}, u32[]{:S(2)}, u32[]{:S(2)}) collective-permute-start(bf16[16,6,80]{2,1,0:T(8,128)(2,1)S(1)} %reshape.357), channel_id=1, source_target_pairs={{511,0},{0,1},{1,2},{2,3},{3,4},{4,5},{5,6},{6,7},{7,8},{8,9},{9,1... | collective-permute-start | bytes 46088 | tf_op jit(solution)/shard_map/ppermute | solution.py:16
  155.4 8.9 %collective-permute-start.17 = (bf16[16,6,80]{2,1,0:T(8,128)(2,1)S(1)}, bf16[16,6,80]{2,1,0:T(8,128)(2,1)S(1)}, u32[]{:S(2)}, u32[]{:S(2)}) collective-permute-start(bf16[16,6,80]{2,1,0:T(8,128)(2,1)S(1)} %reshape.361), channel_id=1, source_target_pairs={{1,0},{2,1},{3,2},{4,3},{5,4},{6,5},{7,6},{8,7},{9,8},{10,9},{11,1... | collective-permute-start | bytes 46088 | tf_op jit(solution)/shard_map/ppermute | solution.py:16
  162.2 5.8 %collective-permute-start.16 = (bf16[16,6,80]{2,1,0:T(8,128)(2,1)S(1)}, bf16[16,6,80]{2,1,0:T(8,128)(2,1)S(1)}, u32[]{:S(2)}, u32[]{:S(2)}) collective-permute-start(bf16[16,6,80]{2,1,0:T(8,128)(2,1)S(1)} %reshape.361), channel_id=1, source_target_pairs={{511,0},{0,1},{1,2},{2,3},{3,4},{4,5},{5,6},{6,7},{7,8},{8,9},{9,1... | collective-permute-start | bytes 46088 | tf_op jit(solution)/shard_map/ppermute | solution.py:16
  173.4 8.7 %collective-permute-start.19 = (bf16[16,6,80]{2,1,0:T(8,128)(2,1)S(1)}, bf16[16,6,80]{2,1,0:T(8,128)(2,1)S(1)}, u32[]{:S(2)}, u32[]{:S(2)}) collective-permute-start(bf16[16,6,80]{2,1,0:T(8,128)(2,1)S(1)} %reshape.365), channel_id=1, source_target_pairs={{1,0},{2,1},{3,2},{4,3},{5,4},{6,5},{7,6},{8,7},{9,8},{10,9},{11,1... | collective-permute-start | bytes 46088 | tf_op jit(solution)/shard_map/ppermute | solution.py:16
  180.2 5.8 %collective-permute-start.18 = (bf16[16,6,80]{2,1,0:T(8,128)(2,1)S(1)}, bf16[16,6,80]{2,1,0:T(8,128)(2,1)S(1)}, u32[]{:S(2)}, u32[]{:S(2)}) collective-permute-start(bf16[16,6,80]{2,1,0:T(8,128)(2,1)S(1)} %reshape.365), channel_id=1, source_target_pairs={{511,0},{0,1},{1,2},{2,3},{3,4},{4,5},{5,6},{6,7},{7,8},{8,9},{9,1... | collective-permute-start | bytes 46088 | tf_op jit(solution)/shard_map/ppermute | solution.py:16
  188.0 8.4 %collective-permute-start.20 = (f32[8,320]{1,0:T(8,128)S(1)}, f32[8,320]{1,0:T(8,128)S(1)}, u32[]{:S(2)}, u32[]{:S(2)}) collective-permute-start(f32[8,320]{1,0:T(8,128)S(1)} %fusion.144), channel_id=1, source_target_pairs={{0,1},{1,0},{2,3},{3,2},{4,5},{5,4},{6,7},{7,6},{8,9},{9,8},{10,11... | collective-permute-start | bytes 30728 | tf_op jit(solution)/shard_map/ppermute | solution.py:154
  196.5 7.1 %collective-permute-start.21 = (f32[8,320]{1,0:T(8,128)S(1)}, f32[8,320]{1,0:T(8,128)S(1)}, u32[]{:S(2)}, u32[]{:S(2)}) collective-permute-start(f32[8,320]{1,0:T(8,128)S(1)} %add.620), channel_id=1, source_target_pairs={{0,2},{1,3},{2,0},{3,1},{4,6},{5,7},{6,4},{7,5},{8,10},{9,11},{10,... | collective-permute-start | bytes 30728 | tf_op jit(solution)/shard_map/ppermute | solution.py:154
  204.6 4.3 %collective-permute-start.23 = (bf16[8,6,80]{2,1,0:T(8,128)(2,1)S(1)}, bf16[8,6,80]{2,1,0:T(8,128)(2,1)S(1)}, u32[]{:S(2)}, u32[]{:S(2)}) collective-permute-start(bf16[8,6,80]{2,1,0:T(8,128)(2,1)S(1)} %reshape.369), channel_id=1, source_target_pairs={{4,0},{8,4},{12,8},{16,12},{20,16},{24,20},{28,24},{32,28},{36,32}... | collective-permute-start | bytes 23048 | tf_op jit(solution)/shard_map/ppermute | solution.py:16
  206.5 8.4 %collective-permute-start.22 = (bf16[8,6,80]{2,1,0:T(8,128)(2,1)S(1)}, bf16[8,6,80]{2,1,0:T(8,128)(2,1)S(1)}, u32[]{:S(2)}, u32[]{:S(2)}) collective-permute-start(bf16[8,6,80]{2,1,0:T(8,128)(2,1)S(1)} %reshape.369), channel_id=1, source_target_pairs={{508,0},{0,4},{4,8},{8,12},{12,16},{16,20},{20,24},{24,28},{28,32}... | collective-permute-start | bytes 23048 | tf_op jit(solution)/shard_map/ppermute | solution.py:16
  217.6 4.3 %collective-permute-start.25 = (bf16[8,6,80]{2,1,0:T(8,128)(2,1)S(1)}, bf16[8,6,80]{2,1,0:T(8,128)(2,1)S(1)}, u32[]{:S(2)}, u32[]{:S(2)}) collective-permute-start(bf16[8,6,80]{2,1,0:T(8,128)(2,1)S(1)} %reshape.373), channel_id=1, source_target_pairs={{4,0},{8,4},{12,8},{16,12},{20,16},{24,20},{28,24},{32,28},{36,32}... | collective-permute-start | bytes 23048 | tf_op jit(solution)/shard_map/ppermute | solution.py:16
  219.6 8.4 %collective-permute-start.24 = (bf16[8,6,80]{2,1,0:T(8,128)(2,1)S(1)}, bf16[8,6,80]{2,1,0:T(8,128)(2,1)S(1)}, u32[]{:S(2)}, u32[]{:S(2)}) collective-permute-start(bf16[8,6,80]{2,1,0:T(8,128)(2,1)S(1)} %reshape.373), channel_id=1, source_target_pairs={{508,0},{0,4},{4,8},{8,12},{12,16},{16,20},{20,24},{24,28},{28,32}... | collective-permute-start | bytes 23048 | tf_op jit(solution)/shard_map/ppermute | solution.py:16
Sparse Core Ops, SparseCore 0:
  21.1 38.3 all-gather.2
